TPU v7x, 128 devices: a whole 4x4x4 slice. The times are simulated.
128 devices in a mesh: rows: 8 (over z_hi, y), cols: 16 (over z_lo, x, core).
Axes of the slice: x: 4, y: 4, z: 4 (z_hi: 2, z_lo: 2; z = z_hi * 2 + z_lo), core: 2. Of those that a mesh axis runs over, the one named last changes fastest.
Arguments:
- dosage: int32 [512, 24576], P('cols', 'rows'), may hold values from 0 to 2
- present: int32 [512, 24576], P('cols', 'rows'), may hold values from 0 to 1, as said below
- components: float32 [32, 24576], P(None, 'rows'), may hold values from -8 to 8
Outputs:
- kinship: float32 [24576, 24576], P('rows', 'cols')
Inputs may be any that keep to these rules, and one draw needn't show every extreme that they name: `present`: markers whose index is a multiple of 8 are observed for every person.
All inputs are finite; a program needn't handle non-finite values.
Results may differ from a plain program's by a relative error of at most 0.0036.
Values may be sent and summed in bfloat16 or wider, within the bound.
A program may use at most 128 MiB of HBM per device.

v0:
```python
import jax
import jax.numpy as jnp
from jax import lax
from jax.sharding import PartitionSpec as P


def broadcast(block, axis, holder):
    block = jnp.where(lax.axis_index(axis) == holder, block, jnp.zeros_like(block))
    return lax.psum(block, axis)


def solve_normal(gram, moment):
    width = gram.shape[0]
    index_col = jnp.arange(width, dtype=jnp.int32)[:, None]
    columns = []
    for j in range(width):
        column = gram[:, j, :]
        if j > 0:
            stacked = jnp.stack(columns, axis=1)
            column = column - jnp.sum(stacked * stacked[j][None, :, :], axis=1)
        pivot = jnp.sqrt(column[j])
        columns.append(jnp.where(index_col >= j, column / pivot[None, :], jnp.zeros_like(column)))
    factor = jnp.stack(columns, axis=1)
    forward = []
    for j in range(width):
        value = moment[j]
        for k in range(j):
            value = value - factor[j, k] * forward[k]
        forward.append(value / factor[j, j])
    backward = [None] * width
    for j in range(width - 1, -1, -1):
        value = forward[j]
        for k in range(j + 1, width):
            value = value - factor[k, j] * backward[k]
        backward[j] = value / factor[j, j]
    return jnp.stack(backward, axis=0)


def per_device(dosage, present, components):
    people = components.shape[1]
    design = jnp.concatenate([jnp.ones((1, people), jnp.float32), components], axis=0)
    width = design.shape[0]
    observed = present.astype(jnp.float32)
    counts = dosage.astype(jnp.float32)
    target = 0.5 * counts * observed
    outer_rows = (design[:, None, :] * design[None, :, :]).reshape(width * width, people)
    gram_part = jnp.dot(
        outer_rows, observed.T, precision=lax.Precision.HIGHEST, preferred_element_type=jnp.float32
    )
    moment_part = jnp.dot(
        design, target.T, precision=lax.Precision.HIGHEST, preferred_element_type=jnp.float32
    )
    gram_flat, moment = lax.psum((gram_part, moment_part), "rows")
    markers_here = observed.shape[0]
    gram = gram_flat.reshape(width, width, markers_here)
    coef = solve_normal(gram, moment)
    fitted = jnp.dot(
        coef.T, design, precision=lax.Precision.HIGHEST, preferred_element_type=jnp.float32
    )
    freq = jnp.clip(fitted, 0.01, 0.99)
    resid = observed * (counts - 2.0 * freq)
    sdev = observed * jnp.sqrt(freq * (1.0 - freq))
    panel = jnp.stack([resid, sdev]).astype(jnp.bfloat16)
    ratio = lax.axis_size("cols") // lax.axis_size("rows")
    column_width = people // ratio
    col_index = lax.axis_index("cols")
    col_start = col_index % ratio * column_width
    owner = col_index // ratio
    contract = (((0,), (0,)), ((), ()))
    full_rows = lax.all_gather(panel, "cols", axis=1, tiled=True)
    own_part = lax.dynamic_slice_in_dim(full_rows, col_start, column_width, 2)
    full_cols = broadcast(own_part, "rows", owner)
    numer = lax.dot_general(
        full_rows[0], full_cols[0], contract, preferred_element_type=jnp.float32
    )
    denom = lax.dot_general(
        full_rows[1], full_cols[1], contract, preferred_element_type=jnp.float32
    )
    return numer / (4.0 * denom)


def solution(mesh):
    placed = (P("cols", "rows"), P("cols", "rows"), P(None, "rows"))
    return jax.shard_map(
        per_device, mesh=mesh, in_specs=placed, out_specs=P("rows", "cols"), check_vma=False
    )
```

profile of v0, /device:TPU:0, one launch (start us, length us, event | category | flops | bytes accessed | tf_op | source)
XLA Modules:
  0.0 338.4 jit_solution(12750329239006864521)
XLA Ops:
  6.5 1.0 concatenate.3
  7.6 8.0 %broadcast_multiply_fusion = f32[33,33,3072]{2,1,0:T(8,128)} fusion(f32[33,3072]{1,0:T(8,128)S(1)} %concatenate.3), kind=kLoop, calls=%fused_computation.1 | loop fusion | flops 3345408 | bytes 13787136 | tf_op jit(solution)/shard_map/mul | solution.py:46
  15.6 10.5 %mul.11354 = f32[1089,3072]{1,0:T(8,128)} reshape(f32[33,33,3072]{2,1,0:T(8,128)} %broadcast_multiply_fusion) | data formatting | bytes 26763264 | tf_op jit(solution)/shard_map/mul | solution.py:46
  26.1 14.2 %fusion.8 = f32[1089,32]{0,1:T(8,128)S(1)} fusion(f32[1089,3072]{1,0:T(8,128)} %mul.11354, s32[32,3072]{1,0:T(8,128)S(1)} %copy-done.1), kind=kOutput, calls=%fused_computation.550 | convolution fusion | flops 1284734976 | bytes 13914240 | tf_op jit(solution)/shard_map/dot_general | solution.py:47
  40.6 1.2 copy.48
  43.4 42.9 %psum.21 = f32[33,32]{1,0:T(8,128)S(1)} all-reduce(f32[33,32]{1,0:T(8,128)S(1)} %fusion.4), channel_id=1, replica_groups=mesh['rows'=8,'cols'=16] {'rows'}, use_global_device_ids=true, to_apply=%region_0.0 | all-reduce | flops 1056 | bytes 8448 | tf_op jit(solution)/shard_map/psum | solution.py:53
  86.4 44.7 %all-reduce.4.cloned.1.call-done = f32[33,33,32]{2,0,1:T(8,128)} async-done(((f32[33,33,32]{2,0,1:T(8,128)}), f32[33,33,32]{2,0,1:T(8,128)}) %all-reduce.4.cloned.1.call-update) | async-done | bytes 139408 | tf_op jit(solution)/shard_map/psum | solution.py:53
  135.0 0.8 constant_dynamic-update-slice_fusion.79
  136.7 0.8 constant_dynamic-update-slice_fusion.514
  138.4 0.8 constant_dynamic-update-slice_fusion.513
  140.1 0.8 constant_dynamic-update-slice_fusion.512
  141.8 0.8 constant_dynamic-update-slice_fusion.511
  143.5 0.8 constant_dynamic-update-slice_fusion.510
  145.2 0.8 constant_dynamic-update-slice_fusion.509
  146.9 0.8 constant_dynamic-update-slice_fusion.508
  148.6 0.8 constant_dynamic-update-slice_fusion.507
  157.1 0.8 fusion.144
  158.4 0.8 subtract_divide_fusion
  160.1 0.8 pad_maximum_fusion
  161.2 40.2 %all-gather.2.cloned.1.call-done = bf16[2,512,3072]{2,1,0:T(8,128)(2,1)} async-done(((bf16[2,32,3072]{2,1,0:T(8,128)(2,1)}), bf16[2,512,3072]{2,1,0:T(8,128)(2,1)}) %all-gather.2.cloned.1.call-update) | async-done | bytes 6291472 | tf_op jit(solution)/shard_map/all_gather | solution.py:70
  201.4 4.1 %dynamic-slice_select_fusion = bf16[2,512,1536]{2,1,0:T(8,128)(2,1)} fusion(bf16[2,512,3072]{2,1,0:T(8,128)(2,1)} %all-gather.2.cloned.1.call-done, s32[]{:T(128)S(6)} %select_n.281, pred[]{:T(512)S(6)} %eq.5), kind=kLoop, calls=%fused_computation.6 | loop fusion | flops 1572864 | bytes 6291461 | tf_op jit(solution)/shard_map/jit(_where)/select_n | solution.py:8
  205.5 100.6 %all-reduce.6.cloned.1.call-done = bf16[2,512,1536]{2,1,0:T(8,128)(2,1)} async-done(((bf16[2,512,1536]{2,1,0:T(8,128)(2,1)}), bf16[2,512,1536]{2,1,0:T(8,128)(2,1)}) %all-reduce.6.cloned.1.call-update) | async-done | bytes 3145744 | tf_op jit(solution)/shard_map/psum | solution.py:9
  306.1 11.7 %fusion = f32[3072,1536]{1,0:T(8,128)} fusion(bf16[2,512,3072]{2,1,0:T(8,128)(2,1)} %all-gather.2.cloned.1.call-done, bf16[2,512,1536]{2,1,0:T(8,128)(2,1)} %all-reduce.6.cloned.1.call-done), kind=kOutput, calls=%fused_computation.5 | convolution fusion | flops 4831838208 | bytes 23592960 | tf_op jit(solution)/shard_map/dot_general | solution.py:73
  317.8 14.1 %multiply_divide_fusion = f32[3072,1536]{1,0:T(8,128)} fusion(f32[3072,1536]{1,0:T(8,128)} %fusion, bf16[2,512,3072]{2,1,0:T(8,128)(2,1)} %all-gather.2.cloned.1.call-done, bf16[2,512,1536]{2,1,0:T(8,128)(2,1)S(1)} %copy-done.4), kind=kOutput, calls=%fused_computation | convolution fusion | flops 4841275392 | bytes 42467328 | tf_op jit(solution)/shard_map/dot_general | solution.py:76
  (305 shorter events, 21.0 us)
Async XLA Ops:
  6.5 124.5 %all-reduce.4.cloned.1.call-start = ((), (), s32[]{:S(2)}) async-start(), calls=%async_computation | async-start | bytes 1351680 | tf_op jit(solution)/shard_map/psum | solution.py:53
  15.6 10.6 %copy-start.1 = (s32[32,3072]{1,0:T(8,128)S(1)}, s32[32,3072]{1,0:T(8,128)}, u32[]{:S(2)}) copy-start(s32[32,3072]{1,0:T(8,128)} %param.4) | copy-start | bytes 1179652
  26.1 16.1 %copy-start = (f32[32,3072]{1,0:T(8,128)S(1)}, f32[32,3072]{1,0:T(8,128)}, u32[]{:S(2)}) copy-start(f32[32,3072]{1,0:T(8,128)} %param.5) | copy-start | bytes 1179652
  26.1 16.1 %copy-start.3 = (s32[32,3072]{1,0:T(8,128)S(1)}, s32[32,3072]{1,0:T(8,128)}, u32[]{:S(2)}) copy-start(s32[32,3072]{1,0:T(8,128)} %param.3) | copy-start | bytes 1179652
  41.8 159.6 %all-gather.2.cloned.1.call-start = ((), (), s32[]{:S(2)}) async-start(), calls=%async_computation.1 | async-start | bytes 6684672 | tf_op jit(solution)/shard_map/all_gather | solution.py:70
  131.1 18.4 %copy-start.2 = (f32[33,33,32]{2,0,1:T(8,128)S(1)}, f32[33,33,32]{2,0,1:T(8,128)}, u32[]{:S(2)}) copy-start(f32[33,33,32]{2,0,1:T(8,128)} %all-reduce.4.cloned.1.call-done) | copy-start | bytes 418180
  160.9 145.2 %all-reduce.6.cloned.1.call-start = ((), (), s32[]{:S(2)}) async-start(), calls=%async_computation.2 | async-start | bytes 6291456 | tf_op jit(solution)/shard_map/psum | solution.py:9
  306.1 11.7 %copy-start.4 = (bf16[2,512,1536]{2,1,0:T(8,128)(2,1)S(1)}, bf16[2,512,1536]{2,1,0:T(8,128)(2,1)}, u32[]{:S(2)}) copy-start(bf16[2,512,1536]{2,1,0:T(8,128)(2,1)} %all-reduce.6.cloned.1.call-done) | copy-start | bytes 9437188
Sparse Core Ops, SparseCore 0:
  41.9 89.0 all-reduce.3
  161.0 40.3 all-gather.1
  205.6 100.4 all-reduce.5
where the time goes:
time: 340 us; the launch traced here: 338 us
  waiting for transfers between devices  186 us (55%)
  blocking collectives  42.9 us (13%)
  matrix products  41.3 us (12%)
  other arithmetic  37.7 us (11%)
  local copies, waits for them, and re-layouts  16.1 us (5%)
  between operations  14.5 us (4%)
    psum x1, waiting for transfers between devices, broadcast(): return lax.psum(block, axis)  101 us
    psum x1, waiting for transfers between devices, per_device(): gram_flat, moment = lax.psum((gram_part, moment_part), 'rows')  44.7 us
    psum x1, blocking collectives, per_device(): gram_flat, moment = lax.psum((gram_part, moment_part), 'rows')  42.9 us
    all_gather x1, waiting for transfers between devices, per_device(): full_rows = lax.all_gather(panel, 'cols', axis=1, tiled=True)  40.2 us
    dot_general x1, matrix products, per_device(): jnp.dot(outer_rows, observed.T, precision=lax.Precision.HIGHEST, preferre...  14.2 us
    dot_general x1, matrix products, per_device(): lax.dot_general(full_rows[1], full_cols[1], contract, preferred_element_t...  14.1 us
    dot_general x1, matrix products, per_device(): lax.dot_general(full_rows[0], full_cols[0], contract, preferred_element_t...  11.7 us
    mul x1, local copies, waits for them, and re-layouts, per_device(): design[:, None, :] * design[None, :, :]  10.5 us
  transfers between devices with their start and end apart: 3, of which 3 were waited for; matrix products, arithmetic and copies ran while one was open for 0% of the time, Pallas kernels for 0%

commit v1 on v0

--- a/solution.py
+++ b/solution.py
@@ -6,7 +6,7 @@
 
 def broadcast(block, axis, holder):
     block = jnp.where(lax.axis_index(axis) == holder, block, jnp.zeros_like(block))
-    return lax.psum(block, axis)
+    return jnp.sum(lax.all_gather(block, axis), axis=0)
 
 
 def solve_normal(gram, moment):

time: 340 us -> 516 us (1.52)
  waiting for transfers between devices: 186 us -> 348 us
  other arithmetic: 37.7 us -> 51.5 us
    all_gather x0 -> x1, waiting for transfers between devices: none -> 263 us  [broadcast(): return jnp.sum(lax.all_gather(block, axis), axis=0)]
    psum x1 -> x0, waiting for transfers between devices: 101 us -> none  [broadcast(): return lax.psum(block, axis)]
    reduce_sum x0 -> x1, other arithmetic: none -> 13.8 us  [broadcast(): return jnp.sum(lax.all_gather(block, axis), axis=0)]
where the time goes in v1:
time: 516 us; the launch traced here: 515 us
  waiting for transfers between devices  348 us (67%)
  other arithmetic  51.5 us (10%)
  blocking collectives  42.9 us (8%)
  matrix products  41.1 us (8%)
  local copies, waits for them, and re-layouts  16.1 us (3%)
  between operations  14.6 us (3%)
    all_gather x1, waiting for transfers between devices, broadcast(): return jnp.sum(lax.all_gather(block, axis), axis=0)  263 us
    psum x1, waiting for transfers between devices, per_device(): gram_flat, moment = lax.psum((gram_part, moment_part), 'rows')  44.7 us
    psum x1, blocking collectives, per_device(): gram_flat, moment = lax.psum((gram_part, moment_part), 'rows')  42.9 us
    all_gather x1, waiting for transfers between devices, per_device(): full_rows = lax.all_gather(panel, 'cols', axis=1, tiled=True)  40.2 us
    dot_general x1, matrix products, per_device(): lax.dot_general(full_rows[1], full_cols[1], contract, preferred_element_t...  14.2 us
    dot_general x1, matrix products, per_device(): jnp.dot(outer_rows, observed.T, precision=lax.Precision.HIGHEST, preferre...  14.2 us
    reduce_sum x1, other arithmetic, broadcast(): return jnp.sum(lax.all_gather(block, axis), axis=0)  13.8 us
    dot_general x1, matrix products, per_device(): lax.dot_general(full_rows[0], full_cols[0], contract, preferred_element_t...  11.4 us
  transfers between devices with their start and end apart: 3, of which 3 were waited for; matrix products, arithmetic and copies ran while one was open for 0% of the time, Pallas kernels for 0%

profile of v1, /device:TPU:0, one launch (start us, length us, event | category | flops | bytes accessed | tf_op | source)
XLA Modules:
  0.0 514.9 jit_solution(12552472655689058030)
XLA Ops:
  6.5 1.0 concatenate.3
  7.6 8.0 %broadcast_multiply_fusion = f32[33,33,3072]{2,1,0:T(8,128)} fusion(f32[33,3072]{1,0:T(8,128)S(1)} %concatenate.3), kind=kLoop, calls=%fused_computation.1 | loop fusion | flops 3345408 | bytes 13787136 | tf_op jit(solution)/shard_map/mul | solution.py:46
  15.6 10.5 %mul.11354 = f32[1089,3072]{1,0:T(8,128)} reshape(f32[33,33,3072]{2,1,0:T(8,128)} %broadcast_multiply_fusion) | data formatting | bytes 26763264 | tf_op jit(solution)/shard_map/mul | solution.py:46
  26.1 14.2 %fusion.8 = f32[1089,32]{0,1:T(8,128)S(1)} fusion(f32[1089,3072]{1,0:T(8,128)} %mul.11354, s32[32,3072]{1,0:T(8,128)S(1)} %copy-done.1), kind=kOutput, calls=%fused_computation.550 | convolution fusion | flops 1284734976 | bytes 13914240 | tf_op jit(solution)/shard_map/dot_general | solution.py:47
  40.5 1.2 copy.70
  43.4 42.9 %psum.14 = f32[33,32]{1,0:T(8,128)S(1)} all-reduce(f32[33,32]{1,0:T(8,128)S(1)} %fusion.4), channel_id=1, replica_groups=mesh['rows'=8,'cols'=16] {'rows'}, use_global_device_ids=true, to_apply=%region_0.0 | all-reduce | flops 1056 | bytes 8448 | tf_op jit(solution)/shard_map/psum | solution.py:53
  86.4 44.7 %all-reduce.3.cloned.1.call-done = f32[33,33,32]{2,0,1:T(8,128)} async-done(((f32[33,33,32]{2,0,1:T(8,128)}), f32[33,33,32]{2,0,1:T(8,128)}) %all-reduce.3.cloned.1.call-update) | async-done | bytes 139408 | tf_op jit(solution)/shard_map/psum | solution.py:53
  135.0 0.8 constant_dynamic-update-slice_fusion.79
  136.7 0.8 constant_dynamic-update-slice_fusion.514
  138.4 0.8 constant_dynamic-update-slice_fusion.513
  140.1 0.8 constant_dynamic-update-slice_fusion.512
  141.8 0.8 constant_dynamic-update-slice_fusion.511
  143.5 0.8 constant_dynamic-update-slice_fusion.510
  145.2 0.8 constant_dynamic-update-slice_fusion.509
  146.9 0.8 constant_dynamic-update-slice_fusion.508
  148.6 0.8 constant_dynamic-update-slice_fusion.507
  157.1 0.8 fusion.144
  158.4 0.8 subtract_divide_fusion
  161.2 40.2 %all-gather.4.cloned.1.call-done = bf16[2,512,3072]{2,1,0:T(8,128)(2,1)} async-done(((bf16[2,32,3072]{2,1,0:T(8,128)(2,1)}), bf16[2,512,3072]{2,1,0:T(8,128)(2,1)}) %all-gather.4.cloned.1.call-update) | async-done | bytes 6291472 | tf_op jit(solution)/shard_map/all_gather | solution.py:70
  201.4 4.1 dynamic-slice_select_fusion
  205.5 263.4 %all-gather.6.cloned.1.call-done = bf16[16,512,1536]{2,1,0:T(8,128)(2,1)} async-done(((bf16[2,512,1536]{2,1,0:T(8,128)(2,1)}), bf16[16,512,1536]{2,1,0:T(8,128)(2,1)}) %all-gather.6.cloned.1.call-update) | async-done | bytes 25165840 | tf_op jit(solution)/shard_map/all_gather | solution.py:9
  468.9 13.8 %reduce_sum.416 = bf16[2,512,1536]{2,1,0:T(8,128)(2,1)S(1)} reduce(bf16[8,2,512,1536]{3,2,1,0:T(8,128)(2,1)} %bitcast.7583, bf16[]{:T(256)} %constant.119.clone.1), dimensions={0}, to_apply=%region_33.34 | reduce | flops 11010048 | bytes 28311554 | tf_op jit(solution)/shard_map/reduce_sum | solution.py:9
  482.7 11.4 %fusion = f32[3072,1536]{1,0:T(8,128)} fusion(bf16[2,512,3072]{2,1,0:T(8,128)(2,1)} %all-gather.4.cloned.1.call-done, bf16[2,512,1536]{2,1,0:T(8,128)(2,1)S(1)} %reduce_sum.416), kind=kOutput, calls=%fused_computation.5 | convolution fusion | flops 4831838208 | bytes 23592960 | tf_op jit(solution)/shard_map/dot_general | solution.py:73
  494.2 14.2 %multiply_divide_fusion = f32[3072,1536]{1,0:T(8,128)} fusion(f32[3072,1536]{1,0:T(8,128)} %fusion, bf16[2,512,3072]{2,1,0:T(8,128)(2,1)} %all-gather.4.cloned.1.call-done, bf16[2,512,1536]{2,1,0:T(8,128)(2,1)S(1)} %reduce_sum.416), kind=kOutput, calls=%fused_computation | convolution fusion | flops 4841275392 | bytes 42467328 | tf_op jit(solution)/shard_map/dot_general | solution.py:76
  (304 shorter events, 21.7 us)
Async XLA Ops:
  6.5 124.5 %all-reduce.3.cloned.1.call-start = ((), (), s32[]{:S(2)}) async-start(), calls=%async_computation | async-start | bytes 1351680 | tf_op jit(solution)/shard_map/psum | solution.py:53
  15.6 10.6 %copy-start.1 = (s32[32,3072]{1,0:T(8,128)S(1)}, s32[32,3072]{1,0:T(8,128)}, u32[]{:S(2)}) copy-start(s32[32,3072]{1,0:T(8,128)} %param.4) | copy-start | bytes 1179652
  26.1 16.1 %copy-start = (f32[32,3072]{1,0:T(8,128)S(1)}, f32[32,3072]{1,0:T(8,128)}, u32[]{:S(2)}) copy-start(f32[32,3072]{1,0:T(8,128)} %param.5) | copy-start | bytes 1179652
  26.1 16.1 %copy-start.3 = (s32[32,3072]{1,0:T(8,128)S(1)}, s32[32,3072]{1,0:T(8,128)}, u32[]{:S(2)}) copy-start(s32[32,3072]{1,0:T(8,128)} %param.3) | copy-start | bytes 1179652
  41.8 159.6 %all-gather.4.cloned.1.call-start = ((), (), s32[]{:S(2)}) async-start(), calls=%async_computation.1 | async-start | bytes 6684672 | tf_op jit(solution)/shard_map/all_gather | solution.py:70
  131.0 18.4 %copy-start.2 = (f32[33,33,32]{2,0,1:T(8,128)S(1)}, f32[33,33,32]{2,0,1:T(8,128)}, u32[]{:S(2)}) copy-start(f32[33,33,32]{2,0,1:T(8,128)} %all-reduce.3.cloned.1.call-done) | copy-start | bytes 418180
  160.9 308.1 %all-gather.6.cloned.1.call-start = ((), (), s32[]{:S(2)}) async-start(), calls=%async_computation.2 | async-start | bytes 28311552 | tf_op jit(solution)/shard_map/all_gather | solution.py:9
Sparse Core Ops, SparseCore 0:
  41.9 89.0 all-reduce.2
  161.0 40.3 all-gather.3
  205.6 263.2 all-gather.5
